TPU v7x, 256 devices: a whole 4x4x8 slice. The times are simulated.
256 devices in a mesh: comp: 2 (over x_lo), face: 128 (over y, z, x_hi, core).
Axes of the slice: x: 4 (x_hi: 2, x_lo: 2; x = x_hi * 2 + x_lo), y: 4, z: 8, core: 2. Of those that a mesh axis runs over, the one named last changes fastest.
Arguments:
- state: bfloat16 [2, 16, 32768], P('comp', None, 'face'), may hold values from -6 to 6
- cotangent: bfloat16 [2, 16, 32768], P('comp', None, 'face'), may hold values from -6 to 6
- land_sea: int32 [32768], P('face'), may hold values 0 or 1
- turn_table: int32 [128, 4], replicated, may hold values from 0 to 3
- first_kernel: bfloat16 [2, 216, 256], P('comp'), may hold values from -0.625 to 0.625
- mid_kernel: bfloat16 [2, 2304, 256], P('comp'), may hold values from -0.1875 to 0.1875
- out_kernel: bfloat16 [2, 2304, 16], P('comp'), may hold values from -0.1875 to 0.1875
- first_gates: int32 [2, 216, 64], P('comp'), may hold values from 0 to 5
- mid_gates: int32 [2, 2304, 64], P('comp'), may hold values from 0 to 5
- out_gates: int32 [2, 2304, 4], P('comp'), may hold values from 0 to 5
Outputs:
- upcoming_climate_estimate: bfloat16 [2, 16, 32768], P('comp', None, 'face')
- condition_adjoint_grid: float32 [2, 16, 32768], P('comp', None, 'face')
- opening_filter_adjoint: float32 [2, 216, 256], P('comp')
- central_filter_adjoint: float32 [2, 589824], P('comp', 'face')
- closing_filter_adjoint: float32 [2, 36864], P('comp', 'face')
Inputs may be any that keep to these rules, and one draw needn't show every extreme that they name: `mid_gates`: a gate value picks one of the six ways of keeping 2 of 4 consecutive output channels. `first_gates`: a gate value picks one of the six ways of keeping 2 of 4 consecutive output channels. `out_gates`: a gate value picks one of the six ways of keeping 2 of 4 consecutive output channels.
All inputs are finite; a program needn't handle non-finite values. No bound on the sum of `land_sea` on one device may be relied on, other than what follows from the above.
Results may differ from a plain program's by a relative error of at most 0.0052.
Values may be sent and summed in bfloat16 or wider, within the bound.
No kernel may reach another device: no remote copies, remote signals or barrier semaphores. Data moves between devices by JAX's collectives and lax.ppermute only.
A program may use at most 64 MiB of HBM per device.

v0:
```python
import jax
import jax.numpy as jnp
from jax import lax
from jax.sharding import PartitionSpec as P

FIELDS = 16
COUPLED = 8
ROW_TILES = 4
TS = 16
EDGE_MAP = (
    ((0, False), (2, True), (1, True), (3, False)),
    ((1, False), (3, True), (0, True), (2, False)),
    ((2, False), (1, False), (3, True), (0, True)),
    ((3, False), (0, False), (2, True), (1, True)),
)


def shifted(value, axis, steps):
    count = lax.axis_size(axis)
    pairs = [(source, (source + steps) % count) for source in range(count)]
    return lax.ppermute(value, axis, pairs)


def partner_2(block, axis, distance):
    count = lax.axis_size(axis)
    route = []
    for low in range(count):
        high = low | 1 << distance
        if high != low and high < count:
            route += [(low, high), (high, low)]
    return lax.ppermute(block, axis, route)


def gate_pair(gates):
    low = (gates >= 3).astype(jnp.int32) + (gates >= 5).astype(jnp.int32)
    high = jnp.where(gates == 0, 1, jnp.where((gates == 1) | (gates == 3), 2, 3)).astype(jnp.int32)
    return (low, high)


def gate_keep(gates):
    low, high = gate_pair(gates)
    lanes = jnp.arange(4, dtype=jnp.int32)
    keep = (low[..., None] == lanes) | (high[..., None] == lanes)
    return keep.reshape(gates.shape[0], gates.shape[1] * 4)


def raw_edges(square):
    return (square[:, :, -1], square[:, :, 0], square[:, -1, :], square[:, 0, :])


def take_edge(square, turn, side):
    edges = raw_edges(square)
    picked = jnp.zeros_like(edges[0])
    for turns in range(4):
        slot, flip = EDGE_MAP[side][turns]
        candidate = edges[slot][:, ::-1] if flip else edges[slot]
        picked = jnp.where(turn == turns, candidate, picked)
    return picked


def add_strip(slots, strip, turn, side):
    slots = list(slots)
    for turns in range(4):
        slot, flip = EDGE_MAP[side][turns]
        candidate = strip[:, ::-1] if flip else strip
        slots[slot] = slots[slot] + jnp.where(turn == turns, candidate, 0.0)
    return slots


def turn_for(turn_table, offset, side):
    here = lax.axis_index("face")
    count = lax.axis_size("face")
    return turn_table[jnp.remainder(here + offset, count), side]


def with_halo(square, turn_table):
    west = shifted(take_edge(square, turn_for(turn_table, 1, 0), 0), "face", 1)
    east = shifted(take_edge(square, turn_for(turn_table, -1, 1), 1), "face", -1)
    south = shifted(take_edge(square, turn_for(turn_table, ROW_TILES, 2), 2), "face", ROW_TILES)
    north = shifted(take_edge(square, turn_for(turn_table, -ROW_TILES, 3), 3), "face", -ROW_TILES)
    padded = jnp.pad(square, ((0, 0), (1, 1), (1, 1)))
    padded = padded.at[:, 1:-1, 0].set(west)
    padded = padded.at[:, 1:-1, -1].set(east)
    padded = padded.at[:, 0, 1:-1].set(south)
    padded = padded.at[:, -1, 1:-1].set(north)
    return padded


def without_halo(dpad, turn_table):
    breadth_count = dpad.shape[1] - 2
    inner = dpad[:, 1:-1, 1:-1]
    slots = [jnp.zeros((dpad.shape[0], breadth_count), jnp.float32) for index in range(4)]
    from_east = shifted(dpad[:, 1:-1, 0], "face", -1)
    slots = add_strip(slots, from_east, turn_for(turn_table, 1, 0), 0)
    from_west = shifted(dpad[:, 1:-1, -1], "face", 1)
    slots = add_strip(slots, from_west, turn_for(turn_table, -1, 1), 1)
    from_north = shifted(dpad[:, 0, 1:-1], "face", -ROW_TILES)
    slots = add_strip(slots, from_north, turn_for(turn_table, ROW_TILES, 2), 2)
    from_south = shifted(dpad[:, -1, 1:-1], "face", ROW_TILES)
    slots = add_strip(slots, from_south, turn_for(turn_table, -ROW_TILES, 3), 3)
    inner = inner.at[:, :, -1].add(slots[0])
    inner = inner.at[:, :, 0].add(slots[1])
    inner = inner.at[:, -1, :].add(slots[2])
    inner = inner.at[:, 0, :].add(slots[3])
    return inner.reshape(inner.shape[0], breadth_count * breadth_count)


def unfold(padded, breadth_count):
    feature_depth = padded.shape[0]
    return jnp.concatenate(
        [
            padded[
                :,
                vertical_place : vertical_place + breadth_count,
                horizontal_place : horizontal_place + breadth_count,
            ].reshape(feature_depth, breadth_count * breadth_count)
            for vertical_place in range(3)
            for horizontal_place in range(3)
        ],
        0,
    )


def fold(columns, feature_depth, breadth_count):
    prognosis_outcome = jnp.zeros(
        (feature_depth, breadth_count + 2, breadth_count + 2), jnp.float32
    )
    index = 0
    for vertical_place in range(3):
        for horizontal_place in range(3):
            square_piece = columns[index * feature_depth : (index + 1) * feature_depth].reshape(
                feature_depth, breadth_count, breadth_count
            )
            prognosis_outcome = prognosis_outcome.at[
                :,
                vertical_place : vertical_place + breadth_count,
                horizontal_place : horizontal_place + breadth_count,
            ].add(square_piece)
            index = index + 1
    return prognosis_outcome


def convolve_stencil(kernel, columns):
    return lax.dot_general(
        kernel, columns, (((0,), (0,)), ((), ())), preferred_element_type=jnp.float32
    )


def kernel_term(columns, grad):
    return lax.dot_general(
        columns, grad, (((1,), (1,)), ((), ())), preferred_element_type=jnp.float32
    )


def slope(values):
    sig = jax.nn.sigmoid(values)
    return sig * (1.0 + values * (1.0 - sig))


def body(
    state,
    cotangent,
    land_sea,
    turn_table,
    first_kernel,
    mid_kernel,
    out_kernel,
    first_gates,
    mid_gates,
    out_gates,
):
    breadth_count = TS
    comp = lax.axis_index("comp")
    zero_half = jnp.zeros((), jnp.bfloat16)
    zero_float = jnp.zeros((), jnp.float32)
    local_region_quantity = state[0]
    partner = partner_2(local_region_quantity[:COUPLED], "comp", 0)
    inputs = jnp.concatenate([local_region_quantity, partner], 0)
    sea = land_sea.astype(jnp.float32)
    scaling_ratio = jnp.where(comp == 1, sea, jnp.ones_like(sea))
    opening_keep = gate_keep(first_gates[0])
    central_keep = gate_keep(mid_gates[0])
    closing_keep = gate_keep(out_gates[0])
    kernel_first = jnp.where(opening_keep, first_kernel[0], zero_half)
    kernel_mid = jnp.where(central_keep, mid_kernel[0], zero_half)
    stencil_produced = jnp.where(closing_keep, out_kernel[0], zero_half)
    in_channels = inputs.shape[0]
    hidden = kernel_mid.shape[1]
    columns_zero = unfold(
        with_halo(inputs.reshape(in_channels, breadth_count, breadth_count), turn_table),
        breadth_count,
    )
    act_one = convolve_stencil(kernel_first, columns_zero)
    hid_one = jax.nn.silu(act_one).astype(jnp.bfloat16)
    columns_one = unfold(
        with_halo(hid_one.reshape(hidden, breadth_count, breadth_count), turn_table), breadth_count
    )
    act_two = convolve_stencil(kernel_mid, columns_one)
    hid_two = jax.nn.silu(act_two).astype(jnp.bfloat16)
    vertical_bands_two = unfold(
        with_halo(hid_two.reshape(hidden, breadth_count, breadth_count), turn_table), breadth_count
    )
    prognosis_outcome = convolve_stencil(stencil_produced, vertical_bands_two)
    upcoming_climate_estimate = (
        local_region_quantity.astype(jnp.float32) + scaling_ratio * prognosis_outcome
    ).astype(jnp.bfloat16)
    cot_float = cotangent[0].astype(jnp.float32)
    grad_three = (scaling_ratio * cot_float).astype(jnp.bfloat16)
    out_local = jnp.where(closing_keep, kernel_term(vertical_bands_two, grad_three), zero_float)
    output_extent = lax.psum_scatter(out_local.reshape(-1), "face", scatter_dimension=0, tiled=True)
    back_two = fold(
        jnp.dot(stencil_produced, grad_three, preferred_element_type=jnp.float32),
        hidden,
        breadth_count,
    )
    grad_hid_two = without_halo(back_two, turn_table)
    grad_two = (grad_hid_two * slope(act_two)).astype(jnp.bfloat16)
    mid_local = jnp.where(central_keep, kernel_term(columns_one, grad_two), zero_float)
    middle_extent = lax.psum_scatter(mid_local.reshape(-1), "face", scatter_dimension=0, tiled=True)
    back_one = fold(
        jnp.dot(kernel_mid, grad_two, preferred_element_type=jnp.float32), hidden, breadth_count
    )
    grad_hid_one = without_halo(back_one, turn_table)
    grad_one = (grad_hid_one * slope(act_one)).astype(jnp.bfloat16)
    first_local = jnp.where(opening_keep, kernel_term(columns_zero, grad_one), zero_float)
    back_zero = fold(
        jnp.dot(kernel_first, grad_one, preferred_element_type=jnp.float32),
        in_channels,
        breadth_count,
    )
    grad_inputs = without_halo(back_zero, turn_table)
    returned = partner_2(grad_inputs[FIELDS:], "comp", 0)
    own_domain_adjoint = cot_float + grad_inputs[:FIELDS]
    own_domain_adjoint = own_domain_adjoint.at[:COUPLED].add(returned)
    leading_gate_total = lax.psum(first_local, "face")
    return (
        upcoming_climate_estimate[None],
        own_domain_adjoint[None],
        leading_gate_total[None],
        middle_extent[None],
        output_extent[None],
    )


def solution(mesh):
    in_specs = (
        P("comp", None, "face"),
        P("comp", None, "face"),
        P("face"),
        P(),
        P("comp", None, None),
        P("comp", None, None),
        P("comp", None, None),
        P("comp", None, None),
        P("comp", None, None),
        P("comp", None, None),
    )
    out_specs = (
        P("comp", None, "face"),
        P("comp", None, "face"),
        P("comp", None, None),
        P("comp", "face"),
        P("comp", "face"),
    )
    return jax.shard_map(body, mesh=mesh, in_specs=in_specs, out_specs=out_specs, check_vma=False)
```

profile of v0, /device:TPU:1, one launch (start us, length us, event | category | flops | bytes accessed | tf_op | source)
XLA Modules:
  0.0 1451.6 jit_solution(15934643901630702702)
XLA Ops:
  7.2 1.3 slice_bitcast_fusion.10
  8.5 2.0 collective-permute-start
  12.9 1.4 fusion.12
  16.2 1.4 copy_add_fusion.1
  17.6 1.6 scatter-add.135
  19.2 2.2 add_select_fusion.1
  21.4 1.7 scatter-add.136
  27.6 8.0 collective-permute-start.15
  39.8 1.9 eq.457
  41.7 2.0 copy.620
  43.7 1.8 eq.466
  45.6 3.4 eq.467
  49.0 3.1 copy.621
  52.3 2.1 compare_or_fusion
  55.1 1.4 constant_dynamic-slice_fusion.2
  67.6 3.6 collective-permute-start.1
  72.0 4.8 collective-permute-start.4
  78.7 4.0 scatter.41
  82.7 5.0 scatter.44
  87.7 3.7 scatter.45
  94.5 6.1 collective-permute-start.6
  100.6 5.0 collective-permute-start.8
  108.6 2.8 collective-permute-start.13
  111.4 1.4 scatter.50
  115.1 2.6 fusion.10
  119.5 2.1 copy_add_fusion
  121.7 2.5 scatter-add.156
  124.1 3.2 add_select_fusion
  127.3 1.7 scatter-add.159
  129.0 1.9 slice_add_fusion.5
  130.9 1.2 scatter-add.160
  132.1 1.8 slice_add_fusion.4
  139.3 7.0 collective-permute-start.10
  146.3 4.8 collective-permute-start.12
  151.7 2.6 copy.690
  154.3 1.5 collective-permute-start.20
  155.8 2.7 collective-permute-start.18
  158.9 4.8 collective-permute-start.17
  163.7 1.4 scatter.56
  170.6 1.3 dynamic-slice_add_fusion
  172.2 1.5 scatter-add.179
  173.7 2.1 add_select_fusion.2
  175.8 1.6 scatter-add.180
  180.5 7.5 collective-permute-start.21
  188.2 4.7 collective-permute-start.23
  195.0 2.4 collective-permute-done.25
  197.4 1242.7 %all-reduce.11.cloned.1.call-done = (f32[1,216,256]{2,1,0:T(8,128)}, f32[589824]{0:T(1024)}, f32[36864]{0:T(1024)}) async-done(((f32[1,216,256]{2,1,0:T(8,128)}, f32[589824]{0:T(1024)}, f32[36864]{0:T(1024)}), (f32[1,216,256]{2,1,0:T(8,128)}, f32[589824]{0:T(1024)}, f32[36864]{0:T(1024)})) %all-reduce.11.cloned.1.call-update) | async-done | bytes 2727952 | tf_op jit(solution)/shard_map/psum | solution.py:235
  1442.8 1.6 copy.810
  (344 shorter events, 45.4 us)
Async XLA Ops:
  7.2 1432.9 %all-reduce.11.cloned.1.call-start = ((), (), s32[]{:S(2)}) async-start(), calls=%async_computation | async-start | bytes 5455872 | tf_op jit(solution)/shard_map/psum | solution.py:235
  8.5 57.6 %collective-permute-start = (bf16[8,256]{1,0:T(8,128)(2,1)}, bf16[8,256]{1,0:T(8,128)(2,1)}, u32[]{:S(2)}, u32[]{:S(2)}) collective-permute-start(bf16[8,256]{1,0:T(8,128)(2,1)} %slice_bitcast_fusion.10), channel_id=1, source_target_pairs={{0,128},{128,0},{1,129},{129,1},{2,130},{130,2},{3,131},{131,3},{4... | collective-permute-start | bytes 12296 | tf_op jit(solution)/shard_map/ppermute | solution.py:31
  12.9 1.4 copy-start.22
  25.2 10.3 copy-start.18
  25.8 11.3 copy-start.16
  27.6 85.8 %collective-permute-start.15 = (f32[256,16]{0,1:T(8,128)}, f32[256,16]{0,1:T(8,128)}, u32[]{:S(2)}, u32[]{:S(2)}) collective-permute-start(f32[256,16]{0,1:T(8,128)} %bitcast.260), channel_id=1, source_target_pairs={{0,124},{1,125},{2,126},{3,127},{4,0},{5,1},{6,2},{7,3},{8,4},{9,5... | collective-permute-start | bytes 49160 | tf_op jit(solution)/shard_map/ppermute | solution.py:21
  37.2 2.0 copy-start.4
  49.0 3.2 copy-start.2
  49.0 3.2 copy-start.3
  52.2 2.1 copy-start.5
  52.2 2.1 copy-start.6
  67.6 9.9 collective-permute-start.1
  71.3 6.4 collective-permute-start.2
  71.4 6.5 collective-permute-start.3
  72.0 6.0 collective-permute-start.4
  91.4 1.7 copy-start.14
  92.7 12.8 copy-start.13
  93.1 13.1 copy-start.11
  93.1 13.1 copy-start.17
  93.1 13.1 copy-start.26
  94.5 13.7 collective-permute-start.6
  100.5 7.7 collective-permute-start.5
  100.6 8.0 collective-permute-start.7
  100.6 12.3 collective-permute-start.8
  108.2 6.0 collective-permute-start.16
  108.3 5.8 collective-permute-start.14
  108.6 6.3 collective-permute-start.13
  115.1 2.6 copy-start
  129.0 6.1 copy-start.1
  139.3 15.0 %collective-permute-start.10 = (bf16[256,16]{0,1:T(8,128)(2,1)S(1)}, bf16[256,16]{0,1:T(8,128)(2,1)S(1)}, u32[]{:S(2)}, u32[]{:S(2)}) collective-permute-start(bf16[256,16]{0,1:T(8,128)(2,1)S(1)} %get-tuple-element.698), channel_id=1, source_target_pairs={{0,127},{1,0},{2,1},{3,2},{4,3},{5,4},{6,5},{7,6},{8,7},{9,8},{10,... | collective-permute-start | bytes 24584 | tf_op jit(solution)/shard_map/ppermute | solution.py:21
  146.3 9.5 collective-permute-start.9
  146.3 12.6 collective-permute-start.11
  146.3 18.9 %collective-permute-start.12 = (bf16[256,16]{0,1:T(8,128)(2,1)S(1)}, bf16[256,16]{0,1:T(8,128)(2,1)S(1)}, u32[]{:S(2)}, u32[]{:S(2)}) collective-permute-start(bf16[256,16]{0,1:T(8,128)(2,1)S(1)} %get-tuple-element.632), channel_id=1, source_target_pairs={{0,124},{1,125},{2,126},{3,127},{4,0},{5,1},{6,2},{7,3},{8,4},{9,5... | collective-permute-start | bytes 24584 | tf_op jit(solution)/shard_map/ppermute | solution.py:21
  154.3 13.6 collective-permute-start.19
  154.3 13.8 collective-permute-start.20
  155.8 12.2 collective-permute-start.18
  158.9 9.2 collective-permute-start.17
  168.0 1.9 copy-start.15
  179.5 13.4 copy-start.9
  179.6 13.4 copy-start.19
  179.6 13.4 copy-start.24
  180.5 13.6 collective-permute-start.21
  188.1 6.1 collective-permute-start.24
  188.1 5.9 collective-permute-start.22
  188.2 9.1 copy-start.20
  188.2 5.8 collective-permute-start.23
  194.5 2.9 collective-permute-start.25
  197.4 1247.1 %copy-start.21 = (f32[1,16,256]{2,1,0:T(8,128)}, f32[1,16,256]{2,1,0:T(8,128)S(1)}, u32[]{:S(2)}) copy-start(f32[1,16,256]{2,1,0:T(8,128)S(1)} %fusion.32) | copy-start | bytes 49156
  (6 other events, 5.3 us)
Sparse Core Ops, SparseCore 0:
  179.3 1260.7 all-reduce.10
where the time goes:
time: 1460 us; the launch traced here: 1450 us
  waiting for transfers between devices  1250 us (86%)
  local copies, waits for them, and re-layouts  78.6 us (5%)
  starting transfers between devices  66.6 us (5%)
  between operations  27.1 us (2%)
  other arithmetic  25 us (2%)
    psum x1, waiting for transfers between devices, body(): leading_gate_total = lax.psum(first_local, 'face')  1240 us
    ppermute x24, starting transfers between devices, shifted(): return lax.ppermute(value, axis, pairs)  64.2 us
  transfers between devices with their start and end apart: 27, of which 3 were waited for; matrix products, arithmetic and copies ran while one was open for 5% of the time, Pallas kernels for 0%

commit v1 on v0

--- a/solution.py
+++ b/solution.py
@@ -232,7 +232,7 @@
     returned = partner_2(grad_inputs[FIELDS:], "comp", 0)
     own_domain_adjoint = cot_float + grad_inputs[:FIELDS]
     own_domain_adjoint = own_domain_adjoint.at[:COUPLED].add(returned)
-    leading_gate_total = lax.psum(first_local, "face")
+    leading_gate_total = jnp.sum(lax.all_gather(first_local, "face"), axis=0)
     return (
         upcoming_climate_estimate[None],
         own_domain_adjoint[None],

time: 1460 us -> 1620 us (1.11)
  waiting for transfers between devices: 1250 us -> 1400 us
    psum x1 -> x0, waiting for transfers between devices: 1240 us -> none  [body(): leading_gate_total = lax.psum(first_local, 'face')]
    unnamed x1 -> x3, waiting for transfers between devices: 0.02 us -> 1200 us
    all_gather x0 -> x1, waiting for transfers between devices: none -> 191 us  [body(): leading_gate_total = jnp.sum(lax.all_gather(first_local, 'face'), axis=0)]
  transfers between devices with their start and end apart: 27 -> 28, of which waited for: 3 -> 8; matrix products, arithmetic and copies ran while one was open for 5% -> 6% of each run, Pallas kernels for 0% -> 0%
where the time goes in v1:
time: 1620 us; the launch traced here: 1610 us
  waiting for transfers between devices  1400 us (86%)
  local copies, waits for them, and re-layouts  76.9 us (5%)
  starting transfers between devices  68 us (4%)
  other arithmetic  33.5 us (2%)
  between operations  27.9 us (2%)
    unnamed x3, waiting for transfers between devices  1200 us
    all_gather x1, waiting for transfers between devices, body(): leading_gate_total = jnp.sum(lax.all_gather(first_local, 'face'), axis=0)  191 us
    ppermute x24, starting transfers between devices, shifted(): return lax.ppermute(value, axis, pairs)  65.8 us
  transfers between devices with their start and end apart: 28, of which 8 were waited for; matrix products, arithmetic and copies ran while one was open for 6% of the time, Pallas kernels for 0%

profile of v1, /device:TPU:1, one launch (start us, length us, event | category | flops | bytes accessed | tf_op | source)
XLA Modules:
  0.0 1611.9 jit_solution(2960651592427421738)
XLA Ops:
  7.2 1.3 slice_bitcast_fusion.10
  8.5 2.0 collective-permute-start
  13.5 1.4 fusion.11
  16.4 1.4 copy_add_fusion.1
  17.8 1.5 scatter-add.135
  19.3 2.1 add_select_fusion.1
  21.4 1.6 scatter-add.136
  27.5 1.6 collective-permute-start.16
  32.6 1.9 eq.457
  34.5 2.0 copy.620
  36.5 1.8 eq.466
  38.3 3.4 eq.467
  41.8 3.1 copy.621
  45.6 2.0 compare_or_fusion
  47.7 1.5 constant_dynamic-slice_fusion.2
  62.6 1.7 collective-permute-start.3
  64.3 1.5 collective-permute-start.2
  65.8 4.8 collective-permute-start.4
  70.6 2.6 collective-permute-start.1
  75.7 4.0 scatter.41
  79.7 4.9 scatter.44
  84.6 3.7 scatter.45
  91.5 8.2 collective-permute-start.6
  99.6 5.0 collective-permute-start.8
  105.8 7.9 collective-permute-start.13
  114.2 1.4 scatter.50
  118.0 1.9 fusion.9
  120.4 5.4 collective-permute-start.10
  125.8 5.0 collective-permute-start.12
  130.8 1.8 fusion.4
  133.8 2.1 copy_add_fusion
  135.9 2.4 scatter-add.156
  138.4 3.7 add_select_fusion
  142.1 2.5 scatter-add.159
  148.9 2.6 copy.690
  152.1 1.4 scatter.56
  158.4 5.0 collective-permute-start.19
  164.5 2.2 collective-permute-start.18
  174.7 1.2 dynamic-slice_add_fusion
  175.9 1.4 scatter-add.179
  177.3 2.0 add_select_fusion.2
  179.3 1.5 scatter-add.180
  182.4 8.3 collective-permute-start.21
  190.8 4.8 collective-permute-start.23
  197.6 2.8 collective-permute-done.25
  200.4 1199.8 %all-reduce.11.cloned.1.call-done = (f32[589824]{0:T(1024)}, f32[36864]{0:T(1024)}) async-done(((f32[589824]{0:T(1024)}, f32[36864]{0:T(1024)}), (f32[589824]{0:T(1024)}, f32[36864]{0:T(1024)})) %all-reduce.11.cloned.1.call-update) | async-done | bytes 2506768
  1403.0 190.7 %all-gather.3.cloned.1.call-done = f32[27648,256]{1,0:T(8,128)} async-done(((f32[216,256]{1,0:T(8,128)}), f32[27648,256]{1,0:T(8,128)}) %all-gather.3.cloned.1.call-update) | async-done | bytes 28311568 | tf_op jit(solution)/shard_map/all_gather | solution.py:235
  1593.8 11.1 reduce_sum.9
  (351 shorter events, 49.8 us)
Async XLA Ops:
  7.2 1393.1 %all-reduce.11.cloned.1.call-start = ((), (), s32[]{:S(2)}) async-start(), calls=%async_computation.1 | async-start | bytes 5013504
  8.5 52.5 %collective-permute-start = (bf16[8,256]{1,0:T(8,128)(2,1)}, bf16[8,256]{1,0:T(8,128)(2,1)}, u32[]{:S(2)}, u32[]{:S(2)}) collective-permute-start(bf16[8,256]{1,0:T(8,128)(2,1)} %slice_bitcast_fusion.10), channel_id=1, source_target_pairs={{0,128},{128,0},{1,129},{129,1},{2,130},{130,2},{3,131},{131,3},{4... | collective-permute-start | bytes 12296 | tf_op jit(solution)/shard_map/ppermute | solution.py:31
  11.8 3.1 copy-start.25
  25.3 3.8 copy-start.18
  25.7 5.6 copy-start.16
  25.7 6.3 copy-start.3
  27.5 88.6 %collective-permute-start.16 = (f32[256,16]{0,1:T(8,128)}, f32[256,16]{0,1:T(8,128)}, u32[]{:S(2)}, u32[]{:S(2)}) collective-permute-start(f32[256,16]{0,1:T(8,128)} %bitcast.262), channel_id=1, source_target_pairs={{0,4},{1,5},{2,6},{3,7},{4,8},{5,9},{6,10},{7,11},{8,12},{9,13},{1... | collective-permute-start | bytes 49160 | tf_op jit(solution)/shard_map/ppermute | solution.py:21
  41.8 3.1 copy-start.4
  41.8 3.1 copy-start.5
  41.8 3.1 copy-start.26
  60.7 12.6 copy-start.24
  62.6 10.9 collective-permute-start.3
  64.3 10.6 collective-permute-start.2
  65.8 7.7 collective-permute-start.4
  70.6 4.0 collective-permute-start.1
  88.3 1.6 copy-start.14
  90.0 15.3 copy-start.11
  90.0 15.3 copy-start.17
  91.4 22.5 %collective-permute-start.7 = (bf16[256,16]{0,1:T(8,128)(2,1)S(1)}, bf16[256,16]{0,1:T(8,128)(2,1)S(1)}, u32[]{:S(2)}, u32[]{:S(2)}) collective-permute-start(bf16[256,16]{0,1:T(8,128)(2,1)S(1)} %get-tuple-element.698), channel_id=1, source_target_pairs={{0,4},{1,5},{2,6},{3,7},{4,8},{5,9},{6,10},{7,11},{8,12},{9,13},{1... | collective-permute-start | bytes 24584 | tf_op jit(solution)/shard_map/ppermute | solution.py:21
  91.5 13.9 collective-permute-start.6
  99.6 15.9 collective-permute-start.8
  104.6 1.2 collective-permute-start.5
  105.4 11.4 collective-permute-start.15
  105.8 11.0 collective-permute-start.13
  113.9 3.0 collective-permute-start.14
  119.8 12.7 copy-start.7
  120.3 31.8 %collective-permute-start.11 = (bf16[256,16]{0,1:T(8,128)(2,1)S(1)}, bf16[256,16]{0,1:T(8,128)(2,1)S(1)}, u32[]{:S(2)}, u32[]{:S(2)}) collective-permute-start(bf16[256,16]{0,1:T(8,128)(2,1)S(1)} %get-tuple-element.696), channel_id=1, source_target_pairs={{0,4},{1,5},{2,6},{3,7},{4,8},{5,9},{6,10},{7,11},{8,12},{9,13},{1... | collective-permute-start | bytes 24584 | tf_op jit(solution)/shard_map/ppermute | solution.py:21
  120.4 31.4 %collective-permute-start.10 = (bf16[256,16]{0,1:T(8,128)(2,1)S(1)}, bf16[256,16]{0,1:T(8,128)(2,1)S(1)}, u32[]{:S(2)}, u32[]{:S(2)}) collective-permute-start(bf16[256,16]{0,1:T(8,128)(2,1)S(1)} %get-tuple-element.697), channel_id=1, source_target_pairs={{0,127},{1,0},{2,1},{3,2},{4,3},{5,4},{6,5},{7,6},{8,7},{9,8},{10,... | collective-permute-start | bytes 24584 | tf_op jit(solution)/shard_map/ppermute | solution.py:21
  125.8 27.7 %collective-permute-start.12 = (bf16[256,16]{0,1:T(8,128)(2,1)S(1)}, bf16[256,16]{0,1:T(8,128)(2,1)S(1)}, u32[]{:S(2)}, u32[]{:S(2)}) collective-permute-start(bf16[256,16]{0,1:T(8,128)(2,1)S(1)} %get-tuple-element.631), channel_id=1, source_target_pairs={{0,124},{1,125},{2,126},{3,127},{4,0},{5,1},{6,2},{7,3},{8,4},{9,5... | collective-permute-start | bytes 24584 | tf_op jit(solution)/shard_map/ppermute | solution.py:21
  130.8 21.1 %collective-permute-start.9 = (bf16[256,16]{0,1:T(8,128)(2,1)S(1)}, bf16[256,16]{0,1:T(8,128)(2,1)S(1)}, u32[]{:S(2)}, u32[]{:S(2)}) collective-permute-start(bf16[256,16]{0,1:T(8,128)(2,1)S(1)} %select_select_fusion.3), channel_id=1, source_target_pairs={{0,1},{1,2},{2,3},{3,4},{4,5},{5,6},{6,7},{7,8},{8,9},{9,10},{10,1... | collective-permute-start | bytes 24584 | tf_op jit(solution)/shard_map/ppermute | solution.py:21
  135.9 8.7 copy-start.2
  156.3 1437.5 %all-gather.3.cloned.1.call-start = ((), (), s32[]{:S(2)}) async-start(), calls=%async_computation | async-start | bytes 28532736 | tf_op jit(solution)/shard_map/all_gather | solution.py:235
  157.9 11.2 copy-start.10
  158.3 8.4 collective-permute-start.20
  158.4 8.4 collective-permute-start.19
  163.4 4.7 collective-permute-start.17
  164.5 4.7 copy-start.12
  164.5 4.0 collective-permute-start.18
  168.6 3.4 copy-start.15
  181.3 14.2 copy-start.9
  181.3 14.2 copy-start.19
  181.4 14.2 copy-start.23
  182.4 14.4 collective-permute-start.21
  190.7 6.0 collective-permute-start.22
  190.7 6.3 collective-permute-start.24
  190.8 5.9 collective-permute-start.23
  197.5 3.0 collective-permute-start.25
  200.4 1404.4 %copy-start.20 = (f32[1,16,256]{2,1,0:T(8,128)}, f32[1,16,256]{2,1,0:T(8,128)S(1)}, u32[]{:S(2)}) copy-start(f32[1,16,256]{2,1,0:T(8,128)S(1)} %fusion.31) | copy-start | bytes 49156
  (9 other events, 9.2 us)
Sparse Core Ops, SparseCore 0:
  156.4 1243.8 all-reduce.10
  1404.7 189.0 all-gather.2
